TPU v7x, 256 devices: a whole 4x4x8 slice. The times are simulated.
256 devices in a mesh: gx: 32 (over y, z), gy: 8 (over x, core).
Axes of the slice: x: 4, y: 4, z: 8, core: 2. Of those that a mesh axis runs over, the one named last changes fastest.
Arguments:
- densities: bfloat16 [24576, 32, 128], P(('gx', 'gy')), may hold values from -6 to 6
- geometry: float32 [24576, 7, 128], P(('gx', 'gy')), as said below
- near_ids: int32 [24576, 8], P(('gx', 'gy')), may hold values from 0 to 24575, as said below
- basis_in: bfloat16 [24576, 64, 128], P(('gx', 'gy')), may hold values from -0.5 to 0.5
- basis_out: bfloat16 [24576, 64, 128], P(('gx', 'gy')), may hold values from -0.75 to 0.75
- leaf_up: bfloat16 [24576, 64, 64], P(('gx', 'gy')), may hold values from -0.078125 to 0.078125
- leaf_down: bfloat16 [24576, 64, 64], P(('gx', 'gy')), may hold values from -0.75 to 0.75
- leaf_coupling: bfloat16 [24576, 6, 64, 64], P(('gx', 'gy')), may hold values from -0.3125 to 0.3125
- leaf_far: int32 [24576, 6], P(('gx', 'gy')), may hold values from 0 to 24575, as said below
- leaf_count: int32 [24576], P(('gx', 'gy')), may hold values from 1 to 6, as said below
- cluster_up: bfloat16 [256, 64, 64], P(('gx', 'gy')), may hold values from -0.25 to 0.25
- cluster_down: bfloat16 [256, 64, 64], P(('gx', 'gy')), may hold values from -0.75 to 0.75
- cluster_coupling: bfloat16 [256, 6, 64, 64], P(('gx', 'gy')), may hold values from -0.3125 to 0.3125
- cluster_far: int32 [256, 6], P(('gx', 'gy')), may hold values from 0 to 255, as said below
- group_up: bfloat16 [32, 64, 64], replicated, may hold values from -0.375 to 0.375
- group_down: bfloat16 [32, 64, 64], P('gx'), may hold values from -0.75 to 0.75
- group_coupling: bfloat16 [32, 6, 64, 64], P('gx'), may hold values from -0.3125 to 0.3125
- group_far: int32 [32, 6], P('gx'), may hold values from 0 to 31, as said below
- root_coupling: bfloat16 [8, 8, 64, 64], replicated, may hold values from -0.25 to 0.25
Outputs:
- potential: float32 [24576, 32, 128], P(('gx', 'gy'))
Inputs may be any that keep to these rules, and one draw needn't show every extreme that they name: `near_ids`: row l names 8 different leaves of a window of 9 consecutive leaves that contains l, centred on l where the ends allow. `leaf_far`: row l names 6 different leaves held by l's device or its two neighbours in leaf order, none within 4 leaves of l; only the first leaf_count[l] entries are used. `leaf_count`: every device holds a leaf with 6. `cluster_far`: row u names 6 different level-two clusters other than u, of u's group or the two groups beside it. `group_far`: row g names 6 different level-one clusters other than g. `geometry`: rows 0 to 2 hold a panel's centre, rows 3 to 5 its unit normal, row 6 its area, from 0.25 to 2.
All inputs are finite; a program needn't handle non-finite values.
Results may differ from a plain program's by a relative error of at most 0.012.
Values may be sent and summed in bfloat16 or wider, within the bound.
A program may use at most 128 MiB of HBM per device.

v0:
```python
import math
import jax
import jax.numpy as jnp
from jax import lax
from jax.sharding import PartitionSpec as P

REACH = 4
BRANCH = 4
four_pi = 4.0 * math.pi
leaf_block = 8


def padded(cells, sides, width):
    for axis, dim in sides:
        count = lax.axis_size(axis)
        ends = count - 1
        head = lax.slice_in_dim(cells, 0, width, axis=dim)
        tail = lax.slice_in_dim(cells, cells.shape[dim] - width, cells.shape[dim], axis=dim)
        cells = jnp.concatenate(
            [
                lax.ppermute(tail, axis, [(i, (i + 1) % count) for i in range(ends)]),
                cells,
                lax.ppermute(head, axis, [((i + 1) % count, i) for i in range(ends)]),
            ],
            axis=dim,
        )
    return cells


def near_kernel(target, source):
    offsets = [
        target[:, coord_id, :, None, None] - source[:, None, :, coord_id, :]
        for coord_id in range(3)
    ]
    distance = offsets[0] * offsets[0] + offsets[1] * offsets[1] + offsets[2] * offsets[2]
    facing = (
        source[:, None, :, 3, :] * offsets[0]
        + source[:, None, :, 4, :] * offsets[1]
        + source[:, None, :, 5, :] * offsets[2]
    )
    panel_area = source[:, None, :, 6, :]
    spread = distance + panel_area
    return panel_area * facing / (four_pi * spread * jnp.sqrt(spread))


def on_device(
    densities,
    geometry,
    near_ids,
    basis_in,
    basis_out,
    leaf_up,
    leaf_down,
    leaf_coupling,
    leaf_far,
    leaf_count,
    cluster_up,
    cluster_down,
    cluster_coupling,
    cluster_far,
    group_up,
    group_down,
    group_coupling,
    group_far,
    root_coupling,
):
    wide = jnp.float32
    narrow = jnp.bfloat16
    leaves = densities.shape[0]
    coeff_order = basis_in.shape[1]
    columns = densities.shape[1]
    flat = coeff_order * columns
    first_leaf = lax.axis_index(("gx", "gy")) * leaves
    gx_index = lax.axis_index("gx")
    group_size = lax.axis_size("gy")
    groups = lax.axis_size("gx")
    leaf_coeffs = jnp.einsum(
        "lkm,lrm->lkr", basis_in, densities, preferred_element_type=wide
    ).astype(narrow)
    mid_coeffs = jnp.einsum(
        "lik,lkr->ir", leaf_up, leaf_coeffs, preferred_element_type=wide
    ).astype(narrow)
    mid_term = jnp.dot(cluster_up[0], mid_coeffs, preferred_element_type=wide).reshape(1, flat)
    mid_flat = mid_coeffs.reshape(1, flat)
    siblings = lax.all_gather(mid_flat, "gy", axis=0, tiled=True)
    group_sum = lax.psum(mid_term, "gy")
    nearby = padded(siblings, (("gx", 0),), group_size)
    mid_picked = jnp.take(nearby, cluster_far[0] - (gx_index - 1) * group_size, axis=0)
    top_coeffs = lax.all_gather(group_sum.astype(narrow), "gx", axis=0, tiled=True)
    top_block = top_coeffs.reshape(groups, coeff_order, columns)
    root_terms = jnp.einsum("gik,gkr->gir", group_up, top_block, preferred_element_type=wide)
    root_coeffs = jnp.sum(
        root_terms.reshape(groups // BRANCH, BRANCH, coeff_order, columns), axis=1
    ).astype(narrow)
    root_row = lax.dynamic_index_in_dim(root_coupling, gx_index // BRANCH, 0, keepdims=False)
    root_field = jnp.einsum(
        "sik,skr->ir", root_row, root_coeffs, preferred_element_type=wide
    ).astype(narrow)
    top_picked = jnp.take(top_block, group_far[0], axis=0)
    top_field = (
        jnp.einsum("fik,fkr->ir", group_coupling[0], top_picked, preferred_element_type=wide)
        + jnp.dot(group_down[0], root_field, preferred_element_type=wide)
    ).astype(narrow)
    mid_block = mid_picked.reshape(-1, coeff_order, columns)
    mid_field = (
        jnp.einsum("fik,fkr->ir", cluster_coupling[0], mid_block, preferred_element_type=wide)
        + jnp.dot(cluster_down[0], top_field, preferred_element_type=wide)
    ).astype(narrow)
    coeff_rim = padded(leaf_coeffs.reshape(leaves, flat), ((("gx", "gy"), 0),), leaves)
    picked = jnp.take(coeff_rim, leaf_far - (first_leaf - leaves), axis=0).reshape(
        leaves, -1, coeff_order, columns
    )
    live_mask = (lax.broadcasted_iota(jnp.int32, leaf_far.shape, 1) < leaf_count[:, None]).astype(
        narrow
    )
    picked = picked * live_mask[:, :, None, None]
    leaf_field = (
        jnp.einsum("lfik,lfkr->lir", leaf_coupling, picked, preferred_element_type=wide)
        + jnp.einsum("lik,kr->lir", leaf_down, mid_field, preferred_element_type=wide)
    ).astype(narrow)
    far_part = jnp.einsum("lkr,lkm->lrm", leaf_field, basis_out, preferred_element_type=wide)
    values_rim = padded(densities, ((("gx", "gy"), 0),), REACH)
    shape_rim = padded(geometry, ((("gx", "gy"), 0),), REACH)
    near_local = near_ids - (first_leaf - REACH)

    def near_block(pieces):
        target, indices = pieces
        source = jnp.take(shape_rim, indices, axis=0)
        values = jnp.take(values_rim, indices, axis=0)
        kernel = near_kernel(target, source).astype(narrow)
        return jnp.einsum("bmnj,bnrj->brm", kernel, values, preferred_element_type=wide)

    near_part = lax.map(
        near_block,
        (
            geometry.reshape(leaves // leaf_block, leaf_block, 7, -1),
            near_local.reshape(leaves // leaf_block, leaf_block, -1),
        ),
    )
    return far_part + near_part.reshape(far_part.shape)


def solution(mesh):
    return jax.shard_map(
        on_device,
        mesh=mesh,
        in_specs=(
            P(("gx", "gy"), None, None),
            P(("gx", "gy"), None, None),
            P(("gx", "gy"), None),
            P(("gx", "gy"), None, None),
            P(("gx", "gy"), None, None),
            P(("gx", "gy"), None, None),
            P(("gx", "gy"), None, None),
            P(("gx", "gy"), None, None, None),
            P(("gx", "gy"), None),
            P(("gx", "gy")),
            P(("gx", "gy"), None, None),
            P(("gx", "gy"), None, None),
            P(("gx", "gy"), None, None, None),
            P(("gx", "gy"), None),
            P(),
            P("gx", None, None),
            P("gx", None, None, None),
            P("gx", None),
            P(),
        ),
        out_specs=P(("gx", "gy"), None, None),
        check_vma=False,
    )
```

profile of v0, /device:TPU:8, one launch (start us, length us, event | category | flops | bytes accessed | tf_op | source)
XLA Modules:
  0.0 328.0 jit_solution(2928487035204301218)
XLA Ops:
  0.0 2.6 convolution_convert_fusion
  4.9 9.3 %collective-permute-start.1 = (bf16[96,2048]{1,0:T(8,128)(2,1)}, bf16[96,2048]{1,0:T(8,128)(2,1)}, u32[]{:S(2)}, u32[]{:S(2)}) collective-permute-start(bf16[96,2048]{1,0:T(8,128)(2,1)} %copy.66), channel_id=1, source_target_pairs={{1,0},{2,1},{3,2},{4,3},{5,4},{6,5},{7,6},{8,7},{9,8},{10,9},{11,1... | collective-permute-start | bytes 1179656 | tf_op jit(solution)/shard_map/ppermute | solution.py:23
  14.2 1.9 collective-permute-start
  17.4 1.9 collective-permute-start.6
  19.3 8.0 %collective-permute-start.7 = (f32[4,7,128]{2,1,0:T(8,128)S(1)}, f32[4,7,128]{2,1,0:T(8,128)S(1)}, u32[]{:S(2)}, u32[]{:S(2)}) collective-permute-start(f32[4,7,128]{2,1,0:T(8,128)S(1)} %get-tuple-element.83), channel_id=1, source_target_pairs={{1,0},{2,1},{3,2},{4,3},{5,4},{6,5},{7,6},{8,7},{9,8},{10,9},{11,1... | collective-permute-start | bytes 43016 | tf_op jit(solution)/shard_map/ppermute | solution.py:23
  27.3 4.0 %copy.72 = bf16[96,64,64]{2,1,0:T(8,128)(2,1)} copy(bf16[96,64,64]{0,2,1:T(8,128)(2,1)} %param.26) | data formatting | bytes 1572864 | tf_op args[5]
  31.4 2.0 fusion.35
  33.5 12.8 %all-gather = bf16[8,1,2048]{2,1,0:T(2,128)(2,1)S(1)} all-gather(bf16[1,1,2048]{2,1,0:T(2,128)(2,1)S(1)} %reshape.240), channel_id=1, replica_groups=mesh['gx'=32,'gy'=8] {'gy'}, dimensions={0}, use_global_device_ids=true | all-gather | bytes 36864 | tf_op jit(solution)/shard_map/all_gather | solution.py:85
  50.4 24.5 %psum.7 = bf16[1,2048]{1,0:T(2,128)(2,1)S(1)} all-reduce(f32[1,2048]{1,0:T(1,128)S(1)} %reshape.189), channel_id=1, replica_groups=mesh['gx'=32,'gy'=8] {'gy'}, use_global_device_ids=true, to_apply=%region_0.0 | all-reduce | flops 2048 | bytes 12288 | tf_op jit(solution)/shard_map/psum | solution.py:86
  74.9 48.0 %all-gather.1 = bf16[32,1,2048]{2,1,0:T(2,128)(2,1)S(1)} all-gather(bf16[1,1,2048]{2,1,0:T(2,128)(2,1)S(1)} %bitcast.169), channel_id=1, replica_groups=mesh['gx'=32,'gy'=8] {'gx'}, dimensions={0}, use_global_device_ids=true | all-gather | bytes 135168 | tf_op jit(solution)/shard_map/all_gather | solution.py:89
  129.4 4.0 %copy.78 = bf16[96,64,64]{2,1,0:T(8,128)(2,1)} copy(bf16[96,64,64]{0,2,1:T(8,128)(2,1)} %param.27) | data formatting | bytes 1572864 | tf_op args[6]
  133.4 16.1 %copy.71 = bf16[96,6,64,64]{3,2,1,0:T(8,128)(2,1)} copy(bf16[96,6,64,64]{0,3,2,1:T(8,128)(2,1)} %param.28) | data formatting | bytes 9437184 | tf_op args[7]
  149.5 2.4 collective-permute-start.2
  152.0 1.9 collective-permute-start.4
  154.0 8.0 %collective-permute-start.5 = (bf16[4,32,128]{2,1,0:T(8,128)(2,1)S(1)}, bf16[4,32,128]{2,1,0:T(8,128)(2,1)S(1)}, u32[]{:S(2)}, u32[]{:S(2)}) collective-permute-start(bf16[4,32,128]{2,1,0:T(8,128)(2,1)S(1)} %get-tuple-element.81), channel_id=1, source_target_pairs={{1,0},{2,1},{3,2},{4,3},{5,4},{6,5},{7,6},{8,7},{9,8},{10,9},{11,1... | collective-permute-start | bytes 98312 | tf_op jit(solution)/shard_map/ppermute | solution.py:23
  164.7 130.7 %while.10 = (s32[]{:T(128)}, f32[12,8,32,128]{3,2,1,0:T(8,128)}, s32[12,8,8]{2,1,0:T(8,128)}, bf16[104,32,128]{2,1,0:T(8,128)(2,1)S(1)}, f32[104,7,128]{2,1,0:T(...) while((s32[]{:T(128)}, f32[12,8,32,128]{3,2,1,0:T(8,128)}, s32[12,8,8]{2,1,0:T(8,128)}, ...), condition=%wide.region_3.4_spmd, body=%wide.region_2.3_spmd.sunk | while | flops 87352896 | bytes 3410213 | solution.py:133
  169.7 5.9 %fusion.84 = f32[12,8,32,128]{3,2,1,0:T(8,128)} fusion(f32[12,8,32,128]{3,2,1,0:T(8,128)} %get-tuple-element.149, s32[]{:T(128)S(6)} %copy.97, f32[8,8,128]{2,1,0:T(8,128)S(1)} %bitcast.159, f32[8,128]{1,0:T(8,128)} %get-tuple-element.132, f32[8,8,128]{2,1,0:T(8,128)S(1)} %bitcast.160, f32[8,8,128]{2,1,0:T(8,128)S(1)} %bitcast.161, ...), kind=kOutput, calls=%fused_computation.21.clone.1 | convolution fusion | flops 87293952 | bytes 897092 | tf_op jit(solution)/shard_map/while/body/eval_jaxpr/bmnj,bnrj->brm/dot_general | solution.py:131
  180.6 5.9 %fusion.84 = f32[12,8,32,128]{3,2,1,0:T(8,128)} fusion(f32[12,8,32,128]{3,2,1,0:T(8,128)} %get-tuple-element.149, s32[]{:T(128)S(6)} %copy.97, f32[8,8,128]{2,1,0:T(8,128)S(1)} %bitcast.159, f32[8,128]{1,0:T(8,128)} %get-tuple-element.132, f32[8,8,128]{2,1,0:T(8,128)S(1)} %bitcast.160, f32[8,8,128]{2,1,0:T(8,128)S(1)} %bitcast.161, ...), kind=kOutput, calls=%fused_computation.21.clone.1 | convolution fusion | flops 87293952 | bytes 897092 | tf_op jit(solution)/shard_map/while/body/eval_jaxpr/bmnj,bnrj->brm/dot_general | solution.py:131
  191.5 5.9 %fusion.84 = f32[12,8,32,128]{3,2,1,0:T(8,128)} fusion(f32[12,8,32,128]{3,2,1,0:T(8,128)} %get-tuple-element.149, s32[]{:T(128)S(6)} %copy.97, f32[8,8,128]{2,1,0:T(8,128)S(1)} %bitcast.159, f32[8,128]{1,0:T(8,128)} %get-tuple-element.132, f32[8,8,128]{2,1,0:T(8,128)S(1)} %bitcast.160, f32[8,8,128]{2,1,0:T(8,128)S(1)} %bitcast.161, ...), kind=kOutput, calls=%fused_computation.21.clone.1 | convolution fusion | flops 87293952 | bytes 897092 | tf_op jit(solution)/shard_map/while/body/eval_jaxpr/bmnj,bnrj->brm/dot_general | solution.py:131
  202.4 5.9 %fusion.84 = f32[12,8,32,128]{3,2,1,0:T(8,128)} fusion(f32[12,8,32,128]{3,2,1,0:T(8,128)} %get-tuple-element.149, s32[]{:T(128)S(6)} %copy.97, f32[8,8,128]{2,1,0:T(8,128)S(1)} %bitcast.159, f32[8,128]{1,0:T(8,128)} %get-tuple-element.132, f32[8,8,128]{2,1,0:T(8,128)S(1)} %bitcast.160, f32[8,8,128]{2,1,0:T(8,128)S(1)} %bitcast.161, ...), kind=kOutput, calls=%fused_computation.21.clone.1 | convolution fusion | flops 87293952 | bytes 897092 | tf_op jit(solution)/shard_map/while/body/eval_jaxpr/bmnj,bnrj->brm/dot_general | solution.py:131
  213.3 5.9 %fusion.84 = f32[12,8,32,128]{3,2,1,0:T(8,128)} fusion(f32[12,8,32,128]{3,2,1,0:T(8,128)} %get-tuple-element.149, s32[]{:T(128)S(6)} %copy.97, f32[8,8,128]{2,1,0:T(8,128)S(1)} %bitcast.159, f32[8,128]{1,0:T(8,128)} %get-tuple-element.132, f32[8,8,128]{2,1,0:T(8,128)S(1)} %bitcast.160, f32[8,8,128]{2,1,0:T(8,128)S(1)} %bitcast.161, ...), kind=kOutput, calls=%fused_computation.21.clone.1 | convolution fusion | flops 87293952 | bytes 897092 | tf_op jit(solution)/shard_map/while/body/eval_jaxpr/bmnj,bnrj->brm/dot_general | solution.py:131
  224.2 5.9 %fusion.84 = f32[12,8,32,128]{3,2,1,0:T(8,128)} fusion(f32[12,8,32,128]{3,2,1,0:T(8,128)} %get-tuple-element.149, s32[]{:T(128)S(6)} %copy.97, f32[8,8,128]{2,1,0:T(8,128)S(1)} %bitcast.159, f32[8,128]{1,0:T(8,128)} %get-tuple-element.132, f32[8,8,128]{2,1,0:T(8,128)S(1)} %bitcast.160, f32[8,8,128]{2,1,0:T(8,128)S(1)} %bitcast.161, ...), kind=kOutput, calls=%fused_computation.21.clone.1 | convolution fusion | flops 87293952 | bytes 897092 | tf_op jit(solution)/shard_map/while/body/eval_jaxpr/bmnj,bnrj->brm/dot_general | solution.py:131
  235.1 5.9 %fusion.84 = f32[12,8,32,128]{3,2,1,0:T(8,128)} fusion(f32[12,8,32,128]{3,2,1,0:T(8,128)} %get-tuple-element.149, s32[]{:T(128)S(6)} %copy.97, f32[8,8,128]{2,1,0:T(8,128)S(1)} %bitcast.159, f32[8,128]{1,0:T(8,128)} %get-tuple-element.132, f32[8,8,128]{2,1,0:T(8,128)S(1)} %bitcast.160, f32[8,8,128]{2,1,0:T(8,128)S(1)} %bitcast.161, ...), kind=kOutput, calls=%fused_computation.21.clone.1 | convolution fusion | flops 87293952 | bytes 897092 | tf_op jit(solution)/shard_map/while/body/eval_jaxpr/bmnj,bnrj->brm/dot_general | solution.py:131
  246.0 5.9 %fusion.84 = f32[12,8,32,128]{3,2,1,0:T(8,128)} fusion(f32[12,8,32,128]{3,2,1,0:T(8,128)} %get-tuple-element.149, s32[]{:T(128)S(6)} %copy.97, f32[8,8,128]{2,1,0:T(8,128)S(1)} %bitcast.159, f32[8,128]{1,0:T(8,128)} %get-tuple-element.132, f32[8,8,128]{2,1,0:T(8,128)S(1)} %bitcast.160, f32[8,8,128]{2,1,0:T(8,128)S(1)} %bitcast.161, ...), kind=kOutput, calls=%fused_computation.21.clone.1 | convolution fusion | flops 87293952 | bytes 897092 | tf_op jit(solution)/shard_map/while/body/eval_jaxpr/bmnj,bnrj->brm/dot_general | solution.py:131
  256.9 5.9 %fusion.84 = f32[12,8,32,128]{3,2,1,0:T(8,128)} fusion(f32[12,8,32,128]{3,2,1,0:T(8,128)} %get-tuple-element.149, s32[]{:T(128)S(6)} %copy.97, f32[8,8,128]{2,1,0:T(8,128)S(1)} %bitcast.159, f32[8,128]{1,0:T(8,128)} %get-tuple-element.132, f32[8,8,128]{2,1,0:T(8,128)S(1)} %bitcast.160, f32[8,8,128]{2,1,0:T(8,128)S(1)} %bitcast.161, ...), kind=kOutput, calls=%fused_computation.21.clone.1 | convolution fusion | flops 87293952 | bytes 897092 | tf_op jit(solution)/shard_map/while/body/eval_jaxpr/bmnj,bnrj->brm/dot_general | solution.py:131
  267.8 5.9 %fusion.84 = f32[12,8,32,128]{3,2,1,0:T(8,128)} fusion(f32[12,8,32,128]{3,2,1,0:T(8,128)} %get-tuple-element.149, s32[]{:T(128)S(6)} %copy.97, f32[8,8,128]{2,1,0:T(8,128)S(1)} %bitcast.159, f32[8,128]{1,0:T(8,128)} %get-tuple-element.132, f32[8,8,128]{2,1,0:T(8,128)S(1)} %bitcast.160, f32[8,8,128]{2,1,0:T(8,128)S(1)} %bitcast.161, ...), kind=kOutput, calls=%fused_computation.21.clone.1 | convolution fusion | flops 87293952 | bytes 897092 | tf_op jit(solution)/shard_map/while/body/eval_jaxpr/bmnj,bnrj->brm/dot_general | solution.py:131
  278.7 5.9 %fusion.84 = f32[12,8,32,128]{3,2,1,0:T(8,128)} fusion(f32[12,8,32,128]{3,2,1,0:T(8,128)} %get-tuple-element.149, s32[]{:T(128)S(6)} %copy.97, f32[8,8,128]{2,1,0:T(8,128)S(1)} %bitcast.159, f32[8,128]{1,0:T(8,128)} %get-tuple-element.132, f32[8,8,128]{2,1,0:T(8,128)S(1)} %bitcast.160, f32[8,8,128]{2,1,0:T(8,128)S(1)} %bitcast.161, ...), kind=kOutput, calls=%fused_computation.21.clone.1 | convolution fusion | flops 87293952 | bytes 897092 | tf_op jit(solution)/shard_map/while/body/eval_jaxpr/bmnj,bnrj->brm/dot_general | solution.py:131
  289.6 5.9 %fusion.84 = f32[12,8,32,128]{3,2,1,0:T(8,128)} fusion(f32[12,8,32,128]{3,2,1,0:T(8,128)} %get-tuple-element.149, s32[]{:T(128)S(6)} %copy.97, f32[8,8,128]{2,1,0:T(8,128)S(1)} %bitcast.159, f32[8,128]{1,0:T(8,128)} %get-tuple-element.132, f32[8,8,128]{2,1,0:T(8,128)S(1)} %bitcast.160, f32[8,8,128]{2,1,0:T(8,128)S(1)} %bitcast.161, ...), kind=kOutput, calls=%fused_computation.21.clone.1 | convolution fusion | flops 87293952 | bytes 897092 | tf_op jit(solution)/shard_map/while/body/eval_jaxpr/bmnj,bnrj->brm/dot_general | solution.py:131
  296.5 4.3 %fusion.37 = f32[32,96,64]{2,0,1:T(8,128)} fusion(bf16[96,64,64]{2,1,0:T(8,128)(2,1)} %copy.78, f32[32,64]{1,0:T(8,128)S(1)} %convolution_bitcast_fusion.3, bf16[32,64]{1,0:T(8,128)(2,1)} %fusion.33, bf16[1,64,64]{2,1,0:T(8,128)(2,1)} %param.32), kind=kOutput, calls=%fused_computation.60 | convolution fusion | flops 25432064 | bytes 1593344 | tf_op jit(solution)/shard_map/lik,kr->lir/dot_general | solution.py:119
  302.1 4.0 %gather_fusion.2 = bf16[576,2048]{1,0:T(8,128)(2,1)} fusion(bf16[288,2048]{1,0:T(8,128)(2,1)S(1)} %pad_maximum_fusion, s32[1024]{0:T(1024)S(1)} %pad_clamp_fusion.3), kind=kCustom, calls=%fused_computation.2 | custom fusion | bytes 4720896 | tf_op jit(solution)/shard_map/jit(_take)/gather | solution.py:110
  306.1 11.7 %gather.23 = bf16[96,6,64,32]{3,2,1,0:T(8,128)(2,1)} reshape(bf16[576,2048]{1,0:T(8,128)(2,1)} %gather_fusion.2) | data formatting | bytes 4718592 | tf_op jit(solution)/shard_map/jit(_take)/gather | solution.py:110
  317.8 10.3 %bitcast_add_fusion.1 = f32[96,32,128]{2,1,0:T(8,128)} fusion(f32[12,8,32,128]{3,2,1,0:T(8,128)} %get-tuple-element.37, bf16[96,64,128]{2,1,0:T(8,128)(2,1)S(1)} %copy-done, f32[32,96,64]{2,0,1:T(8,128)S(1)} %copy-done.1, bf16[96,6,64,64]{3,2,1,0:T(8,128)(2,1)} %copy.71, bf16[96,6,64,32]{3,2,1,0:T(8,128)(2,1)} %gather.23, pred[96,6]{1,0:T(8,128)(4,1)S(1)} %copy-done.6, ...), kind=kOutput, calls=%fused_computation.44 | convolution fusion | flops 204472320 | bytes 12584640 | tf_op jit(solution)/shard_map/lkr,lkm->lrm/dot_general | solution.py:121
  (193 shorter events, 79.2 us)
Async XLA Ops:
  0.0 317.8 %copy-start = (bf16[96,64,128]{2,1,0:T(8,128)(2,1)S(1)}, bf16[96,64,128]{2,1,0:T(8,128)(2,1)}, u32[]{:S(2)}) copy-start(bf16[96,64,128]{2,1,0:T(8,128)(2,1)} %param.25) | copy-start | bytes 4718596
  4.9 295.9 %collective-permute-start.1 = (bf16[96,2048]{1,0:T(8,128)(2,1)}, bf16[96,2048]{1,0:T(8,128)(2,1)}, u32[]{:S(2)}, u32[]{:S(2)}) collective-permute-start(bf16[96,2048]{1,0:T(8,128)(2,1)} %copy.66), channel_id=1, source_target_pairs={{1,0},{2,1},{3,2},{4,3},{5,4},{6,5},{7,6},{8,7},{9,8},{10,9},{11,1... | collective-permute-start | bytes 1179656 | tf_op jit(solution)/shard_map/ppermute | solution.py:23
  14.2 286.6 %collective-permute-start = (bf16[96,2048]{1,0:T(8,128)(2,1)}, bf16[96,2048]{1,0:T(8,128)(2,1)}, u32[]{:S(2)}, u32[]{:S(2)}) collective-permute-start(bf16[96,2048]{1,0:T(8,128)(2,1)} %copy.66), channel_id=1, source_target_pairs={{0,1},{1,2},{2,3},{3,4},{4,5},{5,6},{6,7},{7,8},{8,9},{9,10},{10,1... | collective-permute-start | bytes 1179656 | tf_op jit(solution)/shard_map/ppermute | solution.py:21
  17.4 132.2 %collective-permute-start.6 = (f32[4,7,128]{2,1,0:T(8,128)S(1)}, f32[4,7,128]{2,1,0:T(8,128)S(1)}, u32[]{:S(2)}, u32[]{:S(2)}) collective-permute-start(f32[4,7,128]{2,1,0:T(8,128)S(1)} %get-tuple-element.82), channel_id=1, source_target_pairs={{0,1},{1,2},{2,3},{3,4},{4,5},{5,6},{6,7},{7,8},{8,9},{9,10},{10,1... | collective-permute-start | bytes 43016 | tf_op jit(solution)/shard_map/ppermute | solution.py:21
  19.3 29.0 %copy-start.10 = (s32[1,6]{1,0:T(1,128)S(1)}, s32[1,6]{1,0:T(1,128)}, u32[]{:S(2)}) copy-start(s32[1,6]{1,0:T(1,128)} %param.34) | copy-start | bytes 76
  19.3 29.0 %copy-start.11 = (s32[1,6]{1,0:T(1,128)S(1)}, s32[1,6]{1,0:T(1,128)}, u32[]{:S(2)}) copy-start(s32[1,6]{1,0:T(1,128)} %param.38) | copy-start | bytes 76
  19.3 29.8 %copy-start.9 = (s32[96]{0:T(128)S(1)}, s32[96]{0:T(128)}, u32[]{:S(2)}) copy-start(s32[96]{0:T(128)} %param.30) | copy-start | bytes 1156
  19.3 30.5 %copy-start.7 = (s32[96,6]{0,1:T(8,128)S(1)}, s32[96,6]{0,1:T(8,128)}, u32[]{:S(2)}) copy-start(s32[96,6]{0,1:T(8,128)} %param.29) | copy-start | bytes 6916
  19.3 30.8 %copy-start.4 = (bf16[1,64,64]{2,1,0:T(8,128)(2,1)S(1)}, bf16[1,64,64]{2,1,0:T(8,128)(2,1)}, u32[]{:S(2)}) copy-start(bf16[1,64,64]{2,1,0:T(8,128)(2,1)} %param.31) | copy-start | bytes 24580
  19.3 132.6 %collective-permute-start.7 = (f32[4,7,128]{2,1,0:T(8,128)S(1)}, f32[4,7,128]{2,1,0:T(8,128)S(1)}, u32[]{:S(2)}, u32[]{:S(2)}) collective-permute-start(f32[4,7,128]{2,1,0:T(8,128)S(1)} %get-tuple-element.83), channel_id=1, source_target_pairs={{1,0},{2,1},{3,2},{4,3},{5,4},{6,5},{7,6},{8,7},{9,8},{10,9},{11,1... | collective-permute-start | bytes 43016 | tf_op jit(solution)/shard_map/ppermute | solution.py:23
  31.4 92.7 %copy-start.2 = (bf16[32,64,64]{2,1,0:T(8,128)(2,1)S(1)}, bf16[32,64,64]{2,1,0:T(8,128)(2,1)}, u32[]{:S(2)}) copy-start(bf16[32,64,64]{2,1,0:T(8,128)(2,1)} %param.35) | copy-start | bytes 786436
  31.4 93.7 %copy-start.8 = (s32[96,8]{0,1:T(8,128)S(1)}, s32[96,8]{0,1:T(8,128)}, u32[]{:S(2)}) copy-start(s32[96,8]{0,1:T(8,128)} %param.23) | copy-start | bytes 9220
  33.3 92.9 %copy-start.5 = (bf16[1,64,64]{2,1,0:T(8,128)(2,1)S(1)}, bf16[1,64,64]{2,1,0:T(8,128)(2,1)}, u32[]{:S(2)}) copy-start(bf16[1,64,64]{2,1,0:T(8,128)(2,1)} %param.36) | copy-start | bytes 24580
  46.3 107.6 %collective-permute-start.3 = (bf16[8,2048]{1,0:T(8,128)(2,1)S(1)}, bf16[8,2048]{1,0:T(8,128)(2,1)S(1)}, u32[]{:S(2)}, u32[]{:S(2)}) collective-permute-start(bf16[8,2048]{1,0:T(8,128)(2,1)S(1)} %bitcast.165), channel_id=1, source_target_pairs={{8,0},{16,8},{24,16},{32,24},{40,32},{48,40},{56,48},{64,56},{72,6... | collective-permute-start | bytes 98312 | tf_op jit(solution)/shard_map/ppermute | solution.py:23
  149.5 12.5 %collective-permute-start.2 = (bf16[8,2048]{1,0:T(8,128)(2,1)S(1)}, bf16[8,2048]{1,0:T(8,128)(2,1)S(1)}, u32[]{:S(2)}, u32[]{:S(2)}) collective-permute-start(bf16[8,2048]{1,0:T(8,128)(2,1)S(1)} %bitcast.166), channel_id=1, source_target_pairs={{0,8},{8,16},{16,24},{24,32},{32,40},{40,48},{48,56},{56,64},{64,7... | collective-permute-start | bytes 98312 | tf_op jit(solution)/shard_map/ppermute | solution.py:21
  152.0 11.5 %collective-permute-start.4 = (bf16[4,32,128]{2,1,0:T(8,128)(2,1)S(1)}, bf16[4,32,128]{2,1,0:T(8,128)(2,1)S(1)}, u32[]{:S(2)}, u32[]{:S(2)}) collective-permute-start(bf16[4,32,128]{2,1,0:T(8,128)(2,1)S(1)} %get-tuple-element.80), channel_id=1, source_target_pairs={{0,1},{1,2},{2,3},{3,4},{4,5},{5,6},{6,7},{7,8},{8,9},{9,10},{10,1... | collective-permute-start | bytes 98312 | tf_op jit(solution)/shard_map/ppermute | solution.py:21
  154.0 9.5 %collective-permute-start.5 = (bf16[4,32,128]{2,1,0:T(8,128)(2,1)S(1)}, bf16[4,32,128]{2,1,0:T(8,128)(2,1)S(1)}, u32[]{:S(2)}, u32[]{:S(2)}) collective-permute-start(bf16[4,32,128]{2,1,0:T(8,128)(2,1)S(1)} %get-tuple-element.81), channel_id=1, source_target_pairs={{1,0},{2,1},{3,2},{4,3},{5,4},{6,5},{7,6},{8,7},{9,8},{10,9},{11,1... | collective-permute-start | bytes 98312 | tf_op jit(solution)/shard_map/ppermute | solution.py:23
  306.1 11.7 %copy-start.1 = (f32[32,96,64]{2,0,1:T(8,128)S(1)}, f32[32,96,64]{2,0,1:T(8,128)}, u32[]{:S(2)}) copy-start(f32[32,96,64]{2,0,1:T(8,128)} %fusion.37) | copy-start | bytes 2359300
  306.1 11.7 %copy-start.3 = (bf16[96,6]{1,0:T(8,128)(2,1)S(1)}, bf16[96,6]{1,0:T(8,128)(2,1)}, u32[]{:S(2)}) copy-start(bf16[96,6]{1,0:T(8,128)(2,1)} %fusion.49) | copy-start | bytes 3460
  306.1 11.7 %copy-start.6 = (pred[96,6]{1,0:T(8,128)(4,1)S(1)}, pred[96,6]{1,0:T(8,128)(4,1)}, u32[]{:S(2)}) copy-start(pred[96,6]{1,0:T(8,128)(4,1)} %copy.64) | copy-start | bytes 1732
where the time goes:
time: 331 us; the launch traced here: 328 us
  matrix products  94.2 us (28%)
  local copies, waits for them, and re-layouts  90.2 us (27%)
  blocking collectives  85.2 us (26%)
  starting transfers between devices  35.4 us (11%)
  other arithmetic  22.2 us (7%)
    dot_general x12, matrix products, near_block(): jnp.einsum('bmnj,bnrj->brm', kernel, values, preferred_element_type=wide)  70.5 us
    all_gather x1, blocking collectives, on_device(): lax.all_gather(group_sum.astype(narrow), 'gx', axis=0, tiled=True)  48 us
    ppermute x4, starting transfers between devices, padded(): lax.ppermute(head, axis, [((i + 1) % count, i) for i in range(ends)])  27.2 us
    unnamed x30, local copies, waits for them, and re-layouts  25.5 us
    psum x1, blocking collectives, on_device(): group_sum = lax.psum(mid_term, 'gy')  24.5 us
    gather x2, local copies, waits for them, and re-layouts, on_device(): jnp.take(coeff_rim, leaf_far - (first_leaf - leaves), axis=0)  15.6 us
    all_gather x1, blocking collectives, on_device(): siblings = lax.all_gather(mid_flat, 'gy', axis=0, tiled=True)  12.8 us
    dot_general x1, matrix products, on_device(): jnp.einsum('lkr,lkm->lrm', leaf_field, basis_out, preferred_element_type=...  10.3 us
  transfers between devices with their start and end apart: 8, of which 0 were waited for; matrix products, arithmetic and copies ran while one was open for 53% of the time, Pallas kernels for 0%

commit v1 on v0

--- a/solution.py
+++ b/solution.py
@@ -8,6 +8,12 @@
 BRANCH = 4
 four_pi = 4.0 * math.pi
 leaf_block = 8
+
+
+def add_all(x, mesh_axis):
+    parts = lax.all_gather(x, mesh_axis, axis=0, tiled=False)
+    result = parts.sum(axis=0)
+    return result
 
 
 def padded(cells, sides, width):
@@ -83,7 +89,7 @@
     mid_term = jnp.dot(cluster_up[0], mid_coeffs, preferred_element_type=wide).reshape(1, flat)
     mid_flat = mid_coeffs.reshape(1, flat)
     siblings = lax.all_gather(mid_flat, "gy", axis=0, tiled=True)
-    group_sum = lax.psum(mid_term, "gy")
+    group_sum = add_all(mid_term, "gy")
     nearby = padded(siblings, (("gx", 0),), group_size)
     mid_picked = jnp.take(nearby, cluster_far[0] - (gx_index - 1) * group_size, axis=0)
     top_coeffs = lax.all_gather(group_sum.astype(narrow), "gx", axis=0, tiled=True)

time: 331 us -> 313 us (0.946)
  blocking collectives: 85.2 us -> 68.1 us
    psum x1 -> x0, blocking collectives: 24.5 us -> none  [on_device(): group_sum = lax.psum(mid_term, 'gy')]
    all_gather x0 -> x1, blocking collectives: none -> 12.8 us  [add_all(): parts = lax.all_gather(x, mesh_axis, axis=0, tiled=False)]
    all_gather x1, blocking collectives: 48 us -> 42.5 us  [on_device(): lax.all_gather(group_sum.astype(narrow), 'gx', axis=0, tiled=True)]
  transfers between devices with their start and end apart: 8 -> 8, of which waited for: 0 -> 0; matrix products, arithmetic and copies ran while one was open for 53% -> 56% of each run, Pallas kernels for 0% -> 0%
where the time goes in v1:
time: 313 us; the launch traced here: 310 us
  matrix products  94.4 us (30%)
  local copies, waits for them, and re-layouts  89.9 us (29%)
  blocking collectives  68.1 us (22%)
  starting transfers between devices  34.9 us (11%)
  other arithmetic  21.5 us (7%)
    dot_general x12, matrix products, near_block(): jnp.einsum('bmnj,bnrj->brm', kernel, values, preferred_element_type=wide)  70.6 us
    all_gather x1, blocking collectives, on_device(): lax.all_gather(group_sum.astype(narrow), 'gx', axis=0, tiled=True)  42.5 us
    ppermute x4, starting transfers between devices, padded(): lax.ppermute(head, axis, [((i + 1) % count, i) for i in range(ends)])  27.2 us
    unnamed x30, local copies, waits for them, and re-layouts  25.4 us
    gather x2, local copies, waits for them, and re-layouts, on_device(): jnp.take(coeff_rim, leaf_far - (first_leaf - leaves), axis=0)  15.7 us
    all_gather x1, blocking collectives, add_all(): parts = lax.all_gather(x, mesh_axis, axis=0, tiled=False)  12.8 us
    all_gather x1, blocking collectives, on_device(): siblings = lax.all_gather(mid_flat, 'gy', axis=0, tiled=True)  12.8 us
    dot_general x1, matrix products, on_device(): jnp.einsum('lkr,lkm->lrm', leaf_field, basis_out, preferred_element_type=...  10.3 us
  transfers between devices with their start and end apart: 8, of which 0 were waited for; matrix products, arithmetic and copies ran while one was open for 56% of the time, Pallas kernels for 0%

profile of v1, /device:TPU:8, one launch (start us, length us, event | category | flops | bytes accessed | tf_op | source)
XLA Modules:
  0.0 309.5 jit_solution(346814937421259603)
XLA Ops:
  0.0 2.6 convolution_convert_fusion
  5.0 9.3 %collective-permute-start.1 = (bf16[96,2048]{1,0:T(8,128)(2,1)}, bf16[96,2048]{1,0:T(8,128)(2,1)}, u32[]{:S(2)}, u32[]{:S(2)}) collective-permute-start(bf16[96,2048]{1,0:T(8,128)(2,1)} %copy.66), channel_id=1, source_target_pairs={{1,0},{2,1},{3,2},{4,3},{5,4},{6,5},{7,6},{8,7},{9,8},{10,9},{11,1... | collective-permute-start | bytes 1179656 | tf_op jit(solution)/shard_map/ppermute | solution.py:29
  14.2 1.9 collective-permute-start
  17.4 1.9 collective-permute-start.6
  19.4 8.0 %collective-permute-start.7 = (f32[4,7,128]{2,1,0:T(8,128)S(1)}, f32[4,7,128]{2,1,0:T(8,128)S(1)}, u32[]{:S(2)}, u32[]{:S(2)}) collective-permute-start(f32[4,7,128]{2,1,0:T(8,128)S(1)} %get-tuple-element.83), channel_id=1, source_target_pairs={{1,0},{2,1},{3,2},{4,3},{5,4},{6,5},{7,6},{8,7},{9,8},{10,9},{11,1... | collective-permute-start | bytes 43016 | tf_op jit(solution)/shard_map/ppermute | solution.py:29
  27.4 4.0 %copy.72 = bf16[96,64,64]{2,1,0:T(8,128)(2,1)} copy(bf16[96,64,64]{0,2,1:T(8,128)(2,1)} %param.26) | data formatting | bytes 1572864 | tf_op args[5]
  31.4 2.0 fusion.35
  33.6 12.8 %all-gather.1 = bf16[8,1,2048]{2,1,0:T(2,128)(2,1)S(1)} all-gather(bf16[1,1,2048]{2,1,0:T(2,128)(2,1)S(1)} %reshape.248), channel_id=1, replica_groups=mesh['gx'=32,'gy'=8] {'gy'}, dimensions={0}, use_global_device_ids=true | all-gather | bytes 36864 | tf_op jit(solution)/shard_map/all_gather | solution.py:91
  46.3 1.9 collective-permute-start.3
  50.4 12.8 %all_gather.10 = f32[8,1,2048]{2,1,0:T(1,128)S(1)} all-gather(f32[1,1,2048]{2,1,0:T(1,128)S(1)} %all_gather_reshape.3), channel_id=1, replica_groups=mesh['gx'=32,'gy'=8] {'gy'}, dimensions={0}, use_global_device_ids=true | all-gather | bytes 73728 | tf_op jit(solution)/shard_map/all_gather | solution.py:14
  63.3 42.5 %all-gather = bf16[65536]{0:T(1024)(128)(2,1)S(1)} all-gather(bf16[2048]{0:T(1024)(128)(2,1)S(1)} %reduce_sum.18), channel_id=2, replica_groups=mesh['gx'=32,'gy'=8] {'gx'}, dimensions={0}, use_global_device_ids=true | all-gather | bytes 135168 | tf_op jit(solution)/shard_map/all_gather | solution.py:95
  111.5 4.0 %copy.78 = bf16[96,64,64]{2,1,0:T(8,128)(2,1)} copy(bf16[96,64,64]{0,2,1:T(8,128)(2,1)} %param.27) | data formatting | bytes 1572864 | tf_op args[6]
  115.5 16.1 %copy.71 = bf16[96,6,64,64]{3,2,1,0:T(8,128)(2,1)} copy(bf16[96,6,64,64]{0,3,2,1:T(8,128)(2,1)} %param.28) | data formatting | bytes 9437184 | tf_op args[7]
  133.5 1.9 collective-permute-start.4
  135.5 8.0 %collective-permute-start.5 = (bf16[4,32,128]{2,1,0:T(8,128)(2,1)S(1)}, bf16[4,32,128]{2,1,0:T(8,128)(2,1)S(1)}, u32[]{:S(2)}, u32[]{:S(2)}) collective-permute-start(bf16[4,32,128]{2,1,0:T(8,128)(2,1)S(1)} %get-tuple-element.81), channel_id=1, source_target_pairs={{1,0},{2,1},{3,2},{4,3},{5,4},{6,5},{7,6},{8,7},{9,8},{10,9},{11,1... | collective-permute-start | bytes 98312 | tf_op jit(solution)/shard_map/ppermute | solution.py:29
  146.2 130.7 %while.10 = (s32[]{:T(128)}, f32[12,8,32,128]{3,2,1,0:T(8,128)}, s32[12,8,8]{2,1,0:T(8,128)}, bf16[104,32,128]{2,1,0:T(8,128)(2,1)S(1)}, f32[104,7,128]{2,1,0:T(...) while((s32[]{:T(128)}, f32[12,8,32,128]{3,2,1,0:T(8,128)}, s32[12,8,8]{2,1,0:T(8,128)}, ...), condition=%wide.region_3.4_spmd, body=%wide.region_2.3_spmd.sunk | while | flops 87352896 | bytes 3410213 | solution.py:139
  151.2 5.9 %fusion.84 = f32[12,8,32,128]{3,2,1,0:T(8,128)} fusion(f32[12,8,32,128]{3,2,1,0:T(8,128)} %get-tuple-element.149, s32[]{:T(128)S(6)} %copy.97, f32[8,8,128]{2,1,0:T(8,128)S(1)} %bitcast.156, f32[8,128]{1,0:T(8,128)} %get-tuple-element.132, f32[8,8,128]{2,1,0:T(8,128)S(1)} %bitcast.157, f32[8,8,128]{2,1,0:T(8,128)S(1)} %bitcast.158, ...), kind=kOutput, calls=%fused_computation.21.clone.1 | convolution fusion | flops 87293952 | bytes 897092 | tf_op jit(solution)/shard_map/while/body/eval_jaxpr/bmnj,bnrj->brm/dot_general | solution.py:137
  162.1 5.9 %fusion.84 = f32[12,8,32,128]{3,2,1,0:T(8,128)} fusion(f32[12,8,32,128]{3,2,1,0:T(8,128)} %get-tuple-element.149, s32[]{:T(128)S(6)} %copy.97, f32[8,8,128]{2,1,0:T(8,128)S(1)} %bitcast.156, f32[8,128]{1,0:T(8,128)} %get-tuple-element.132, f32[8,8,128]{2,1,0:T(8,128)S(1)} %bitcast.157, f32[8,8,128]{2,1,0:T(8,128)S(1)} %bitcast.158, ...), kind=kOutput, calls=%fused_computation.21.clone.1 | convolution fusion | flops 87293952 | bytes 897092 | tf_op jit(solution)/shard_map/while/body/eval_jaxpr/bmnj,bnrj->brm/dot_general | solution.py:137
  173.0 5.9 %fusion.84 = f32[12,8,32,128]{3,2,1,0:T(8,128)} fusion(f32[12,8,32,128]{3,2,1,0:T(8,128)} %get-tuple-element.149, s32[]{:T(128)S(6)} %copy.97, f32[8,8,128]{2,1,0:T(8,128)S(1)} %bitcast.156, f32[8,128]{1,0:T(8,128)} %get-tuple-element.132, f32[8,8,128]{2,1,0:T(8,128)S(1)} %bitcast.157, f32[8,8,128]{2,1,0:T(8,128)S(1)} %bitcast.158, ...), kind=kOutput, calls=%fused_computation.21.clone.1 | convolution fusion | flops 87293952 | bytes 897092 | tf_op jit(solution)/shard_map/while/body/eval_jaxpr/bmnj,bnrj->brm/dot_general | solution.py:137
  183.9 5.9 %fusion.84 = f32[12,8,32,128]{3,2,1,0:T(8,128)} fusion(f32[12,8,32,128]{3,2,1,0:T(8,128)} %get-tuple-element.149, s32[]{:T(128)S(6)} %copy.97, f32[8,8,128]{2,1,0:T(8,128)S(1)} %bitcast.156, f32[8,128]{1,0:T(8,128)} %get-tuple-element.132, f32[8,8,128]{2,1,0:T(8,128)S(1)} %bitcast.157, f32[8,8,128]{2,1,0:T(8,128)S(1)} %bitcast.158, ...), kind=kOutput, calls=%fused_computation.21.clone.1 | convolution fusion | flops 87293952 | bytes 897092 | tf_op jit(solution)/shard_map/while/body/eval_jaxpr/bmnj,bnrj->brm/dot_general | solution.py:137
  194.8 5.9 %fusion.84 = f32[12,8,32,128]{3,2,1,0:T(8,128)} fusion(f32[12,8,32,128]{3,2,1,0:T(8,128)} %get-tuple-element.149, s32[]{:T(128)S(6)} %copy.97, f32[8,8,128]{2,1,0:T(8,128)S(1)} %bitcast.156, f32[8,128]{1,0:T(8,128)} %get-tuple-element.132, f32[8,8,128]{2,1,0:T(8,128)S(1)} %bitcast.157, f32[8,8,128]{2,1,0:T(8,128)S(1)} %bitcast.158, ...), kind=kOutput, calls=%fused_computation.21.clone.1 | convolution fusion | flops 87293952 | bytes 897092 | tf_op jit(solution)/shard_map/while/body/eval_jaxpr/bmnj,bnrj->brm/dot_general | solution.py:137
  205.7 5.9 %fusion.84 = f32[12,8,32,128]{3,2,1,0:T(8,128)} fusion(f32[12,8,32,128]{3,2,1,0:T(8,128)} %get-tuple-element.149, s32[]{:T(128)S(6)} %copy.97, f32[8,8,128]{2,1,0:T(8,128)S(1)} %bitcast.156, f32[8,128]{1,0:T(8,128)} %get-tuple-element.132, f32[8,8,128]{2,1,0:T(8,128)S(1)} %bitcast.157, f32[8,8,128]{2,1,0:T(8,128)S(1)} %bitcast.158, ...), kind=kOutput, calls=%fused_computation.21.clone.1 | convolution fusion | flops 87293952 | bytes 897092 | tf_op jit(solution)/shard_map/while/body/eval_jaxpr/bmnj,bnrj->brm/dot_general | solution.py:137
  216.6 5.9 %fusion.84 = f32[12,8,32,128]{3,2,1,0:T(8,128)} fusion(f32[12,8,32,128]{3,2,1,0:T(8,128)} %get-tuple-element.149, s32[]{:T(128)S(6)} %copy.97, f32[8,8,128]{2,1,0:T(8,128)S(1)} %bitcast.156, f32[8,128]{1,0:T(8,128)} %get-tuple-element.132, f32[8,8,128]{2,1,0:T(8,128)S(1)} %bitcast.157, f32[8,8,128]{2,1,0:T(8,128)S(1)} %bitcast.158, ...), kind=kOutput, calls=%fused_computation.21.clone.1 | convolution fusion | flops 87293952 | bytes 897092 | tf_op jit(solution)/shard_map/while/body/eval_jaxpr/bmnj,bnrj->brm/dot_general | solution.py:137
  227.5 5.9 %fusion.84 = f32[12,8,32,128]{3,2,1,0:T(8,128)} fusion(f32[12,8,32,128]{3,2,1,0:T(8,128)} %get-tuple-element.149, s32[]{:T(128)S(6)} %copy.97, f32[8,8,128]{2,1,0:T(8,128)S(1)} %bitcast.156, f32[8,128]{1,0:T(8,128)} %get-tuple-element.132, f32[8,8,128]{2,1,0:T(8,128)S(1)} %bitcast.157, f32[8,8,128]{2,1,0:T(8,128)S(1)} %bitcast.158, ...), kind=kOutput, calls=%fused_computation.21.clone.1 | convolution fusion | flops 87293952 | bytes 897092 | tf_op jit(solution)/shard_map/while/body/eval_jaxpr/bmnj,bnrj->brm/dot_general | solution.py:137
  238.4 5.9 %fusion.84 = f32[12,8,32,128]{3,2,1,0:T(8,128)} fusion(f32[12,8,32,128]{3,2,1,0:T(8,128)} %get-tuple-element.149, s32[]{:T(128)S(6)} %copy.97, f32[8,8,128]{2,1,0:T(8,128)S(1)} %bitcast.156, f32[8,128]{1,0:T(8,128)} %get-tuple-element.132, f32[8,8,128]{2,1,0:T(8,128)S(1)} %bitcast.157, f32[8,8,128]{2,1,0:T(8,128)S(1)} %bitcast.158, ...), kind=kOutput, calls=%fused_computation.21.clone.1 | convolution fusion | flops 87293952 | bytes 897092 | tf_op jit(solution)/shard_map/while/body/eval_jaxpr/bmnj,bnrj->brm/dot_general | solution.py:137
  249.3 5.9 %fusion.84 = f32[12,8,32,128]{3,2,1,0:T(8,128)} fusion(f32[12,8,32,128]{3,2,1,0:T(8,128)} %get-tuple-element.149, s32[]{:T(128)S(6)} %copy.97, f32[8,8,128]{2,1,0:T(8,128)S(1)} %bitcast.156, f32[8,128]{1,0:T(8,128)} %get-tuple-element.132, f32[8,8,128]{2,1,0:T(8,128)S(1)} %bitcast.157, f32[8,8,128]{2,1,0:T(8,128)S(1)} %bitcast.158, ...), kind=kOutput, calls=%fused_computation.21.clone.1 | convolution fusion | flops 87293952 | bytes 897092 | tf_op jit(solution)/shard_map/while/body/eval_jaxpr/bmnj,bnrj->brm/dot_general | solution.py:137
  260.2 5.9 %fusion.84 = f32[12,8,32,128]{3,2,1,0:T(8,128)} fusion(f32[12,8,32,128]{3,2,1,0:T(8,128)} %get-tuple-element.149, s32[]{:T(128)S(6)} %copy.97, f32[8,8,128]{2,1,0:T(8,128)S(1)} %bitcast.156, f32[8,128]{1,0:T(8,128)} %get-tuple-element.132, f32[8,8,128]{2,1,0:T(8,128)S(1)} %bitcast.157, f32[8,8,128]{2,1,0:T(8,128)S(1)} %bitcast.158, ...), kind=kOutput, calls=%fused_computation.21.clone.1 | convolution fusion | flops 87293952 | bytes 897092 | tf_op jit(solution)/shard_map/while/body/eval_jaxpr/bmnj,bnrj->brm/dot_general | solution.py:137
  271.0 5.9 %fusion.84 = f32[12,8,32,128]{3,2,1,0:T(8,128)} fusion(f32[12,8,32,128]{3,2,1,0:T(8,128)} %get-tuple-element.149, s32[]{:T(128)S(6)} %copy.97, f32[8,8,128]{2,1,0:T(8,128)S(1)} %bitcast.156, f32[8,128]{1,0:T(8,128)} %get-tuple-element.132, f32[8,8,128]{2,1,0:T(8,128)S(1)} %bitcast.157, f32[8,8,128]{2,1,0:T(8,128)S(1)} %bitcast.158, ...), kind=kOutput, calls=%fused_computation.21.clone.1 | convolution fusion | flops 87293952 | bytes 897092 | tf_op jit(solution)/shard_map/while/body/eval_jaxpr/bmnj,bnrj->brm/dot_general | solution.py:137
  278.0 4.2 %fusion.37 = f32[32,96,64]{2,0,1:T(8,128)} fusion(bf16[96,64,64]{2,1,0:T(8,128)(2,1)} %copy.78, f32[32,64]{1,0:T(8,128)S(1)} %convolution_bitcast_fusion.3, bf16[32,64]{1,0:T(8,128)(2,1)} %fusion.33, bf16[1,64,64]{2,1,0:T(8,128)(2,1)} %param.32), kind=kOutput, calls=%fused_computation.60 | convolution fusion | flops 25432064 | bytes 1593344 | tf_op jit(solution)/shard_map/lik,kr->lir/dot_general | solution.py:125
  283.6 4.0 %gather_fusion.2 = bf16[576,2048]{1,0:T(8,128)(2,1)} fusion(bf16[288,2048]{1,0:T(8,128)(2,1)S(1)} %pad_maximum_fusion, s32[1024]{0:T(1024)S(1)} %pad_clamp_fusion.3), kind=kCustom, calls=%fused_computation.2 | custom fusion | bytes 4720896 | tf_op jit(solution)/shard_map/jit(_take)/gather | solution.py:116
  287.6 11.7 %gather.23 = bf16[96,6,64,32]{3,2,1,0:T(8,128)(2,1)} reshape(bf16[576,2048]{1,0:T(8,128)(2,1)} %gather_fusion.2) | data formatting | bytes 4718592 | tf_op jit(solution)/shard_map/jit(_take)/gather | solution.py:116
  299.3 10.3 %bitcast_add_fusion.1 = f32[96,32,128]{2,1,0:T(8,128)} fusion(f32[12,8,32,128]{3,2,1,0:T(8,128)} %get-tuple-element.37, bf16[96,64,128]{2,1,0:T(8,128)(2,1)S(1)} %copy-done, f32[32,96,64]{2,0,1:T(8,128)S(1)} %copy-done.1, bf16[96,6,64,64]{3,2,1,0:T(8,128)(2,1)} %copy.71, bf16[96,6,64,32]{3,2,1,0:T(8,128)(2,1)} %gather.23, pred[96,6]{1,0:T(8,128)(4,1)S(1)} %copy-done.6, ...), kind=kOutput, calls=%fused_computation.44 | convolution fusion | flops 204472320 | bytes 12584640 | tf_op jit(solution)/shard_map/lkr,lkm->lrm/dot_general | solution.py:127
  (193 shorter events, 78.3 us)
Async XLA Ops:
  0.0 299.3 %copy-start = (bf16[96,64,128]{2,1,0:T(8,128)(2,1)S(1)}, bf16[96,64,128]{2,1,0:T(8,128)(2,1)}, u32[]{:S(2)}) copy-start(bf16[96,64,128]{2,1,0:T(8,128)(2,1)} %param.25) | copy-start | bytes 4718596
  5.0 277.3 %collective-permute-start.1 = (bf16[96,2048]{1,0:T(8,128)(2,1)}, bf16[96,2048]{1,0:T(8,128)(2,1)}, u32[]{:S(2)}, u32[]{:S(2)}) collective-permute-start(bf16[96,2048]{1,0:T(8,128)(2,1)} %copy.66), channel_id=1, source_target_pairs={{1,0},{2,1},{3,2},{4,3},{5,4},{6,5},{7,6},{8,7},{9,8},{10,9},{11,1... | collective-permute-start | bytes 1179656 | tf_op jit(solution)/shard_map/ppermute | solution.py:29
  14.2 268.0 %collective-permute-start = (bf16[96,2048]{1,0:T(8,128)(2,1)}, bf16[96,2048]{1,0:T(8,128)(2,1)}, u32[]{:S(2)}, u32[]{:S(2)}) collective-permute-start(bf16[96,2048]{1,0:T(8,128)(2,1)} %copy.66), channel_id=1, source_target_pairs={{0,1},{1,2},{2,3},{3,4},{4,5},{5,6},{6,7},{7,8},{8,9},{9,10},{10,1... | collective-permute-start | bytes 1179656 | tf_op jit(solution)/shard_map/ppermute | solution.py:27
  17.4 114.2 %collective-permute-start.6 = (f32[4,7,128]{2,1,0:T(8,128)S(1)}, f32[4,7,128]{2,1,0:T(8,128)S(1)}, u32[]{:S(2)}, u32[]{:S(2)}) collective-permute-start(f32[4,7,128]{2,1,0:T(8,128)S(1)} %get-tuple-element.82), channel_id=1, source_target_pairs={{0,1},{1,2},{2,3},{3,4},{4,5},{5,6},{6,7},{7,8},{8,9},{9,10},{10,1... | collective-permute-start | bytes 43016 | tf_op jit(solution)/shard_map/ppermute | solution.py:27
  19.3 29.0 %copy-start.10 = (s32[1,6]{1,0:T(1,128)S(1)}, s32[1,6]{1,0:T(1,128)}, u32[]{:S(2)}) copy-start(s32[1,6]{1,0:T(1,128)} %param.34) | copy-start | bytes 76
  19.3 29.0 %copy-start.11 = (s32[1,6]{1,0:T(1,128)S(1)}, s32[1,6]{1,0:T(1,128)}, u32[]{:S(2)}) copy-start(s32[1,6]{1,0:T(1,128)} %param.38) | copy-start | bytes 76
  19.3 29.9 %copy-start.9 = (s32[96]{0:T(128)S(1)}, s32[96]{0:T(128)}, u32[]{:S(2)}) copy-start(s32[96]{0:T(128)} %param.30) | copy-start | bytes 1156
  19.3 30.5 %copy-start.7 = (s32[96,6]{0,1:T(8,128)S(1)}, s32[96,6]{0,1:T(8,128)}, u32[]{:S(2)}) copy-start(s32[96,6]{0,1:T(8,128)} %param.29) | copy-start | bytes 6916
  19.3 30.8 %copy-start.4 = (bf16[1,64,64]{2,1,0:T(8,128)(2,1)S(1)}, bf16[1,64,64]{2,1,0:T(8,128)(2,1)}, u32[]{:S(2)}) copy-start(bf16[1,64,64]{2,1,0:T(8,128)(2,1)} %param.31) | copy-start | bytes 24580
  19.4 114.1 %collective-permute-start.7 = (f32[4,7,128]{2,1,0:T(8,128)S(1)}, f32[4,7,128]{2,1,0:T(8,128)S(1)}, u32[]{:S(2)}, u32[]{:S(2)}) collective-permute-start(f32[4,7,128]{2,1,0:T(8,128)S(1)} %get-tuple-element.83), channel_id=1, source_target_pairs={{1,0},{2,1},{3,2},{4,3},{5,4},{6,5},{7,6},{8,7},{9,8},{10,9},{11,1... | collective-permute-start | bytes 43016 | tf_op jit(solution)/shard_map/ppermute | solution.py:29
  31.4 74.7 %copy-start.2 = (bf16[32,64,64]{2,1,0:T(8,128)(2,1)S(1)}, bf16[32,64,64]{2,1,0:T(8,128)(2,1)}, u32[]{:S(2)}) copy-start(bf16[32,64,64]{2,1,0:T(8,128)(2,1)} %param.35) | copy-start | bytes 786436
  31.4 75.7 %copy-start.8 = (s32[96,8]{0,1:T(8,128)S(1)}, s32[96,8]{0,1:T(8,128)}, u32[]{:S(2)}) copy-start(s32[96,8]{0,1:T(8,128)} %param.23) | copy-start | bytes 9220
  31.4 76.9 %copy-start.5 = (bf16[1,64,64]{2,1,0:T(8,128)(2,1)S(1)}, bf16[1,64,64]{2,1,0:T(8,128)(2,1)}, u32[]{:S(2)}) copy-start(bf16[1,64,64]{2,1,0:T(8,128)(2,1)} %param.36) | copy-start | bytes 24580
  46.3 89.1 %collective-permute-start.3 = (bf16[8,2048]{1,0:T(8,128)(2,1)S(1)}, bf16[8,2048]{1,0:T(8,128)(2,1)S(1)}, u32[]{:S(2)}, u32[]{:S(2)}) collective-permute-start(bf16[8,2048]{1,0:T(8,128)(2,1)S(1)} %bitcast.162), channel_id=1, source_target_pairs={{8,0},{16,8},{24,16},{32,24},{40,32},{48,40},{56,48},{64,56},{72,6... | collective-permute-start | bytes 98312 | tf_op jit(solution)/shard_map/ppermute | solution.py:29
  131.6 12.0 %collective-permute-start.2 = (bf16[8,2048]{1,0:T(8,128)(2,1)S(1)}, bf16[8,2048]{1,0:T(8,128)(2,1)S(1)}, u32[]{:S(2)}, u32[]{:S(2)}) collective-permute-start(bf16[8,2048]{1,0:T(8,128)(2,1)S(1)} %bitcast.163), channel_id=1, source_target_pairs={{0,8},{8,16},{16,24},{24,32},{32,40},{40,48},{48,56},{56,64},{64,7... | collective-permute-start | bytes 98312 | tf_op jit(solution)/shard_map/ppermute | solution.py:27
  133.5 11.5 %collective-permute-start.4 = (bf16[4,32,128]{2,1,0:T(8,128)(2,1)S(1)}, bf16[4,32,128]{2,1,0:T(8,128)(2,1)S(1)}, u32[]{:S(2)}, u32[]{:S(2)}) collective-permute-start(bf16[4,32,128]{2,1,0:T(8,128)(2,1)S(1)} %get-tuple-element.80), channel_id=1, source_target_pairs={{0,1},{1,2},{2,3},{3,4},{4,5},{5,6},{6,7},{7,8},{8,9},{9,10},{10,1... | collective-permute-start | bytes 98312 | tf_op jit(solution)/shard_map/ppermute | solution.py:27
  135.5 9.5 %collective-permute-start.5 = (bf16[4,32,128]{2,1,0:T(8,128)(2,1)S(1)}, bf16[4,32,128]{2,1,0:T(8,128)(2,1)S(1)}, u32[]{:S(2)}, u32[]{:S(2)}) collective-permute-start(bf16[4,32,128]{2,1,0:T(8,128)(2,1)S(1)} %get-tuple-element.81), channel_id=1, source_target_pairs={{1,0},{2,1},{3,2},{4,3},{5,4},{6,5},{7,6},{8,7},{9,8},{10,9},{11,1... | collective-permute-start | bytes 98312 | tf_op jit(solution)/shard_map/ppermute | solution.py:29
  287.6 11.7 %copy-start.1 = (f32[32,96,64]{2,0,1:T(8,128)S(1)}, f32[32,96,64]{2,0,1:T(8,128)}, u32[]{:S(2)}) copy-start(f32[32,96,64]{2,0,1:T(8,128)} %fusion.37) | copy-start | bytes 2359300
  287.6 11.7 %copy-start.3 = (bf16[96,6]{1,0:T(8,128)(2,1)S(1)}, bf16[96,6]{1,0:T(8,128)(2,1)}, u32[]{:S(2)}) copy-start(bf16[96,6]{1,0:T(8,128)(2,1)} %fusion.49) | copy-start | bytes 3460
  287.6 11.7 %copy-start.6 = (pred[96,6]{1,0:T(8,128)(4,1)S(1)}, pred[96,6]{1,0:T(8,128)(4,1)}, u32[]{:S(2)}) copy-start(pred[96,6]{1,0:T(8,128)(4,1)} %copy.64) | copy-start | bytes 1732
